TPU v7x, 32 devices: a whole 2x2x4 slice. The times are simulated.
32 devices in a mesh: gx: 4 (over x, core), gy: 8 (over z, y).
Axes of the slice: x: 2, y: 2, z: 4, core: 2. Of those that a mesh axis runs over, the one named last changes fastest.
Arguments:
- field: float32 [12, 64, 64, 128], P(None, 'gx', 'gy'), may hold values from -16 to 16
- diffusion: float32 [12], replicated, may hold values from 0.02 to 0.15
- prefactor: float32 [12], replicated, may hold values from 0.05 to 0.3
- activation: float32 [12], replicated, may hold values from 0.5 to 2
- mixing: float32 [12, 12], replicated, may hold values from -1.75 to 1.75
- basis_x: float32 [64, 64], P('gx'), may hold values from -1 to 1, as said below
- basis_y: float32 [64, 64], P('gy'), may hold values from -1 to 1, as said below
- basis_z: float32 [128, 32], replicated, may hold values from -1 to 1, as said below
- basis_v: float32 [12, 6], replicated, may hold values from -1 to 1, as said below
Outputs:
- state: float32 [12, 64, 64, 128], P(None, 'gx', 'gy')
- recon: float32 [12, 64, 64, 128], P(None, 'gx', 'gy')
- residual: float32 [12], replicated
Inputs may be any that keep to these rules, and one draw needn't show every extreme that they name: `basis_x`: its 64 columns are mutually orthogonal, each of norm between 0.5 and 1. `basis_y`: its 64 columns are orthonormal. `basis_z`: its 32 columns are orthonormal. `basis_v`: its 6 columns are orthonormal.
All inputs are finite; a program needn't handle non-finite values.
Results may differ from a plain program's by a relative error of at most 0.00013.
Values sent between devices are 32-bit elements; how exact they have to be, the bound alone decides.
No kernel may reach another device: no remote copies, remote signals or barrier semaphores. Data moves between devices by JAX's collectives and lax.ppermute only.
A program may use at most 64 MiB of HBM per device.

v0:
```python
import jax
import jax.numpy as jnp
from jax import lax
from jax.sharding import PartitionSpec as P

HIGH = lax.Precision.HIGHEST


def padded_2(array, sides, width):
    for axis, dim in sides:
        peers, length = (lax.axis_size(axis), array.shape[dim])
        up = [(i, (i + 1) % peers) for i in range(peers - 1)]
        down = [(j, i) for i, j in up]
        last = lax.slice_in_dim(array, length - width, length, axis=dim)
        first = lax.slice_in_dim(array, 0, width, axis=dim)
        before = lax.ppermute(last, axis, up)
        after = lax.ppermute(first, axis, down)
        array = jnp.concatenate([before, array, after], axis=dim)
    return array


def lap_core(padded):
    centre = padded[:, 1:-1, 1:-1, 1:-1]
    summed = padded[:, 2:, 1:-1, 1:-1] + padded[:, :-2, 1:-1, 1:-1]
    summed = summed + padded[:, 1:-1, 2:, 1:-1] + padded[:, 1:-1, :-2, 1:-1]
    summed = summed + padded[:, 1:-1, 1:-1, 2:] + padded[:, 1:-1, 1:-1, :-2]
    return summed - 6.0 * centre


def reaction(centre, coeffs):
    diffusion, prefactor, activation, mixing = coeffs
    temper = 1.5 + jnp.tanh(centre[0])
    rate_terms = (
        prefactor[:, None, None, None]
        * jnp.exp(-activation[:, None, None, None] / temper[None])
        * centre
    )
    return jnp.einsum("vw,wxyz->vxyz", mixing, rate_terms, precision=HIGH)


def tendency(rimmed, centre, coeffs):
    padded = jnp.pad(rimmed, ((0, 0), (0, 0), (0, 0), (1, 1)))
    return coeffs[0][:, None, None, None] * lap_core(padded) + reaction(centre, coeffs)


def inside_mask(rows_x, rows_y):
    pos_x = lax.axis_index("gx") * rows_x + jnp.arange(rows_x + 2) - 1
    pos_y = lax.axis_index("gy") * rows_y + jnp.arange(rows_y + 2) - 1
    in_x = (pos_x >= 0) & (pos_x < rows_x * lax.axis_size("gx"))
    in_y = (pos_y >= 0) & (pos_y < rows_y * lax.axis_size("gy"))
    return in_x[:, None] & in_y[None, :]


def step_deep(state, coeffs, inside):
    wide = padded_2(state, (("gx", 1), ("gy", 2)), 2)
    centre = wide[:, 1:-1, 1:-1]
    section_wide = centre + tendency(wide, centre, coeffs)
    section_wide = jnp.where(inside[None, :, :, None], section_wide, 0.0)
    section = section_wide[:, 1:-1, 1:-1]
    return 0.5 * (state + section + tendency(section_wide, section, coeffs))


def on_device(field, diffusion, prefactor, activation, mixing, basis_x, basis_y, basis_z, basis_v):
    coeffs = (diffusion, prefactor, activation, mixing)
    rows_x = field.shape[1]
    rows_y = field.shape[2]
    state = field
    inside = inside_mask(rows_x, rows_y)
    state = step_deep(state, coeffs, inside)
    rank_z = basis_z.shape[1]
    rank_v = basis_v.shape[1]
    width = rank_z * rank_v
    proj_z = jnp.einsum("vxyz,zr->vxyr", state, basis_z, precision=HIGH)
    packed = jnp.einsum("vxyr,vs->xyrs", proj_z, basis_v, precision=HIGH)
    packed = packed.reshape(rows_x, rows_y, width)
    columns = basis_x
    part_x = lax.psum_scatter(
        jnp.einsum("xa,xyk->ayk", columns, packed, precision=HIGH),
        "gx",
        scatter_dimension=0,
        tiled=True,
    )
    core_block = jnp.einsum("ayk,yb->abk", part_x, basis_y, precision=HIGH)
    core_block = lax.psum(core_block, "gy")
    mixed_y = jnp.einsum("abk,yb->ayk", core_block, basis_y, precision=HIGH)
    columns = basis_x
    decoded = jnp.einsum(
        "xa,ayk->xyk", columns, lax.all_gather(mixed_y, "gx", axis=0, tiled=True), precision=HIGH
    )
    decoded = decoded.reshape(rows_x, rows_y, rank_z, rank_v)
    back_v = jnp.einsum("xyrs,vs->vxyr", decoded, basis_v, precision=HIGH)
    recon = jnp.einsum("vxyr,zr->vxyz", back_v, basis_z, precision=HIGH)
    error = state - recon
    miss_local = jnp.sum(error * error, axis=(1, 2, 3))
    mass_local = jnp.sum(state * state, axis=(1, 2, 3))
    miss, mass = lax.psum((miss_local, mass_local), ("gx", "gy"))
    residual = jnp.sqrt(miss / (mass + 1e-06))
    return (state, recon, residual)


def solution(mesh):
    return jax.shard_map(
        on_device,
        mesh=mesh,
        in_specs=(
            P(None, "gx", "gy", None),
            P(),
            P(),
            P(),
            P(),
            P("gx", None),
            P("gy", None),
            P(),
            P(),
        ),
        out_specs=(P(None, "gx", "gy", None), P(None, "gx", "gy", None), P()),
        check_vma=False,
    )
```

profile of v0, /device:TPU:0, one launch (start us, length us, event | category | flops | bytes accessed | tf_op | source)
XLA Modules:
  0.0 209.1 jit_solution(7740615977400366910)
XLA Ops:
  7.2 1.0 fusion.57
  8.3 2.4 %collective-permute-start = (f32[12,2,8,128]{3,0,2,1:T(8,128)S(1)}, f32[12,2,8,128]{3,0,2,1:T(8,128)S(1)}, u32[]{:S(2)}, u32[]{:S(2)}) collective-permute-start(f32[12,2,8,128]{3,0,2,1:T(8,128)S(1)} %copy.76), channel_id=1, source_target_pairs={{0,8},{8,16},{16,24},{1,9},{9,17},{17,25},{2,10},{10,18},{18,26},{... | collective-permute-start | bytes 294920 | tf_op jit(solution)/shard_map/ppermute | solution.py:16
  10.8 1.3 collective-permute-start.1
  12.1 0.5 copy_dynamic-update-slice_fusion
  12.6 3.5 %collective-permute-done.1 = f32[12,2,8,128]{3,0,2,1:T(8,128)S(1)} collective-permute-done((f32[12,2,8,128]{3,0,2,1:T(8,128)S(1)}, f32[12,2,8,128]{3,0,2,1:T(8,128)S(1)}, u32[]{:S(2)}, u32[]{:S(2)}) %collective-permute-start.1) | collective-permute-done | bytes 98336 | tf_op jit(solution)/shard_map/ppermute | solution.py:17
  16.2 3.4 %collective-permute-start.2 = (f32[12,20,2,128]{3,0,2,1:T(8,128)S(1)}, f32[12,20,2,128]{3,0,2,1:T(8,128)S(1)}, u32[]{:S(2)}, u32[]{:S(2)}) collective-permute-start(f32[12,20,2,128]{3,0,2,1:T(8,128)S(1)} %get-tuple-element.19), channel_id=1, source_target_pairs={{0,1},{1,2},{2,3},{3,4},{4,5},{5,6},{6,7},{8,9},{9,10},{10,11},{11... | collective-permute-start | bytes 737288 | tf_op jit(solution)/shard_map/ppermute | solution.py:16
  19.6 1.3 collective-permute-start.3
  21.0 4.2 %collective-permute-done.2 = f32[12,20,2,128]{3,0,2,1:T(8,128)S(1)} collective-permute-done((f32[12,20,2,128]{3,0,2,1:T(8,128)S(1)}, f32[12,20,2,128]{3,0,2,1:T(8,128)S(1)}, u32[]{:S(2)}, u32[]{:S(2)}) %collective-permute-start.2) | collective-permute-done | bytes 245792 | tf_op jit(solution)/shard_map/ppermute | solution.py:16
  25.2 4.6 %collective-permute-done.3 = f32[12,20,2,128]{3,0,2,1:T(8,128)S(1)} collective-permute-done((f32[12,20,2,128]{3,0,2,1:T(8,128)S(1)}, f32[12,20,2,128]{3,0,2,1:T(8,128)S(1)}, u32[]{:S(2)}, u32[]{:S(2)}) %collective-permute-start.3) | collective-permute-done | bytes 245792 | tf_op jit(solution)/shard_map/ppermute | solution.py:17
  29.8 0.2 pad_maximum_fusion
  30.0 0.1 fusion.41
  30.1 2.3 %fusion.8 = f32[12,18,10,128]{3,0,2,1:T(8,128)S(1)} fusion(f32[12,20,12,128]{3,0,2,1:T(8,128)S(1)} %pad_maximum_fusion, f32[12,20,8,128]{3,0,2,1:T(8,128)S(1)} %constant_dynamic-update-slice_fusion, f32[12,20,2,128]{3,0,2,1:T(8,128)S(1)} %collective-permute-done.2, f32[12,20,2,128]{3,0,2,1:T(8,128)S(1)} %collective-permute-done.3, ...), kind=kOutput, calls=%fused_computation.14 | convolution fusion | flops 44236800 | bytes 11096576 | tf_op jit(solution)/shard_map/vw,wxyz->vxyz/dot_general | solution.py:38
  32.6 2.2 %fusion.23 = f32[12,16,8,128]{3,0,2,1:T(8,128)S(1)} fusion(f32[12,18,10,128]{3,0,2,1:T(8,128)S(1)} %fusion.8, f32[16,8,128]{2,1,0:T(8,128)S(1)} %bitcast.62, f32[12]{0:T(128)S(1)} %neg.5, f32[12]{0:T(128)S(1)} %copy-done.8, f32[12]{0:T(128)S(1)} %copy-done.9, f32[12,16,8,128]{3,2,1,0:T(8,128)S(1)} %copy-done.2, f32[12,12]{1,0:T(8,128)S(1)} %copy-done.6), kind=kOutput, calls=%fused_computation.37 | convolution fusion | flops 31260672 | bytes 9414144 | tf_op jit(solution)/shard_map/vw,wxyz->vxyz/dot_general | solution.py:38
  34.8 1.0 fusion.44
  35.8 0.7 fusion.51
  36.5 0.5 copy.49
  37.1 1.7 convolution_bitcast_fusion.3
  38.7 1.1 copy.51
  39.9 27.8 %reduce-scatter.2.cloned.1.call-done = f32[16,8,192]{2,1,0:T(8,128)} async-done(((f32[64,8,192]{2,1,0:T(8,128)}), f32[16,8,192]{2,1,0:T(8,128)}) %reduce-scatter.2.cloned.1.call-update) | async-done | bytes 98320 | tf_op jit(solution)/shard_map/reduce_scatter | solution.py:77
  67.7 2.9 %convolution_bitcast_fusion.1 = f32[16,64,192]{2,1,0:T(8,128)} fusion(f32[16,8,192]{2,1,0:T(8,128)} %reduce-scatter.2.cloned.1.call-done, f32[8,64]{1,0:T(8,128)S(1)} %copy-done.4), kind=kOutput, calls=%fused_computation.23 | convolution fusion | flops 18874368 | bytes 886784 | tf_op jit(solution)/shard_map/ayk,yb->abk/dot_general | solution.py:83
  70.6 1.1 copy.57
  71.7 77.8 %all-reduce.5.cloned.1.call-done = f32[16,64,192]{2,1,0:T(8,128)} async-done(((f32[16,64,192]{2,1,0:T(8,128)}), f32[16,64,192]{2,1,0:T(8,128)}) %all-reduce.5.cloned.1.call-update) | async-done | bytes 786448 | tf_op jit(solution)/shard_map/psum | solution.py:84
  149.5 1.9 convolution_bitcast_fusion.5
  151.3 7.3 %all_gather.3 = f32[64,8,192]{2,1,0:T(8,128)S(1)} all-gather(f32[16,8,192]{2,1,0:T(8,128)S(1)} %convolution_bitcast_fusion.5), channel_id=1, replica_groups=mesh['gx'=4,'gy'=8] {'gx'}, dimensions={0}, use_global_device_ids=true | all-gather | bytes 491520 | tf_op jit(solution)/shard_map/all_gather | solution.py:88
  158.7 0.5 convolution_bitcast_fusion.4
  159.2 0.3 copy.53
  159.5 0.6 copy.54
  160.1 1.0 convolution_bitcast_fusion
  161.2 0.9 fusion.31
  162.1 0.7 multiply_reduce_fusion
  162.8 38.9 %all-reduce.2 = (f32[12]{0:T(128)S(1)}, f32[12]{0:T(128)S(1)}) all-reduce(f32[12]{0:T(128)S(1)} %get-tuple-element.16, f32[12]{0:T(128)S(1)} %get-tuple-element.15), channel_id=1, replica_groups=mesh['gx'=4,'gy'=8] {'gx','gy'}, use_global_device_ids=true, to_apply=%region_3.4 | all-reduce | flops 24 | bytes 192 | tf_op jit(solution)/shard_map/psum | solution.py:96
  201.7 0.5 fusion.55
  (36 shorter events, 0.5 us)
Async XLA Ops:
  7.2 27.6 %copy-start = (f32[128,32]{0,1:T(8,128)S(1)}, f32[128,32]{0,1:T(8,128)}, u32[]{:S(2)}) copy-start(f32[128,32]{0,1:T(8,128)} %param.16) | copy-start | bytes 49156
  7.2 4.9 %copy-start.2 = (f32[12,16,8,128]{3,2,1,0:T(8,128)S(1)}, f32[12,16,8,128]{3,2,1,0:T(8,128)}, u32[]{:S(2)}) copy-start(f32[12,16,8,128]{3,2,1,0:T(8,128)} %param.9) | copy-start | bytes 2359300
  7.2 60.5 %reduce-scatter.2.cloned.1.call-start = ((), (), s32[]{:S(2)}) async-start(), calls=%async_computation.1 | async-start | bytes 655360 | tf_op jit(solution)/shard_map/reduce_scatter | solution.py:77
  8.3 3.8 %collective-permute-start = (f32[12,2,8,128]{3,0,2,1:T(8,128)S(1)}, f32[12,2,8,128]{3,0,2,1:T(8,128)S(1)}, u32[]{:S(2)}, u32[]{:S(2)}) collective-permute-start(f32[12,2,8,128]{3,0,2,1:T(8,128)S(1)} %copy.76), channel_id=1, source_target_pairs={{0,8},{8,16},{16,24},{1,9},{9,17},{17,25},{2,10},{10,18},{18,26},{... | collective-permute-start | bytes 294920 | tf_op jit(solution)/shard_map/ppermute | solution.py:16
  10.8 5.3 %collective-permute-start.1 = (f32[12,2,8,128]{3,0,2,1:T(8,128)S(1)}, f32[12,2,8,128]{3,0,2,1:T(8,128)S(1)}, u32[]{:S(2)}, u32[]{:S(2)}) collective-permute-start(f32[12,2,8,128]{3,0,2,1:T(8,128)S(1)} %copy.77), channel_id=1, source_target_pairs={{8,0},{16,8},{24,16},{9,1},{17,9},{25,17},{10,2},{18,10},{26,18},{... | collective-permute-start | bytes 294920 | tf_op jit(solution)/shard_map/ppermute | solution.py:17
  12.1 8.8 %copy-start.7 = (f32[12]{0:T(128)S(1)}, f32[12]{0:T(128)}, u32[]{:S(2)}) copy-start(f32[12]{0:T(128)} %param.12) | copy-start | bytes 148
  16.2 9.0 %collective-permute-start.2 = (f32[12,20,2,128]{3,0,2,1:T(8,128)S(1)}, f32[12,20,2,128]{3,0,2,1:T(8,128)S(1)}, u32[]{:S(2)}, u32[]{:S(2)}) collective-permute-start(f32[12,20,2,128]{3,0,2,1:T(8,128)S(1)} %get-tuple-element.19), channel_id=1, source_target_pairs={{0,1},{1,2},{2,3},{3,4},{4,5},{5,6},{6,7},{8,9},{9,10},{10,11},{11... | collective-permute-start | bytes 737288 | tf_op jit(solution)/shard_map/ppermute | solution.py:16
  19.6 10.2 %collective-permute-start.3 = (f32[12,20,2,128]{3,0,2,1:T(8,128)S(1)}, f32[12,20,2,128]{3,0,2,1:T(8,128)S(1)}, u32[]{:S(2)}, u32[]{:S(2)}) collective-permute-start(f32[12,20,2,128]{3,0,2,1:T(8,128)S(1)} %get-tuple-element.20), channel_id=1, source_target_pairs={{1,0},{2,1},{3,2},{4,3},{5,4},{6,5},{7,6},{9,8},{10,9},{11,10},{12... | collective-permute-start | bytes 737288 | tf_op jit(solution)/shard_map/ppermute | solution.py:17
  21.0 9.1 %copy-start.6 = (f32[12,12]{1,0:T(8,128)S(1)}, f32[12,12]{1,0:T(8,128)}, u32[]{:S(2)}) copy-start(f32[12,12]{1,0:T(8,128)} %param.13) | copy-start | bytes 1732
  21.0 9.1 %copy-start.8 = (f32[12]{0:T(128)S(1)}, f32[12]{0:T(128)}, u32[]{:S(2)}) copy-start(f32[12]{0:T(128)} %param.11) | copy-start | bytes 148
  21.0 9.1 %copy-start.9 = (f32[12]{0:T(128)S(1)}, f32[12]{0:T(128)}, u32[]{:S(2)}) copy-start(f32[12]{0:T(128)} %param.10) | copy-start | bytes 148
  34.8 1.0 copy-start.5
  35.8 1.3 copy-start.3
  37.1 30.6 %copy-start.4 = (f32[8,64]{1,0:T(8,128)S(1)}, f32[8,64]{1,0:T(8,128)}, u32[]{:S(2)}) copy-start(f32[8,64]{1,0:T(8,128)} %param.15) | copy-start | bytes 6148
  39.9 109.6 %all-reduce.5.cloned.1.call-start = ((), (), s32[]{:S(2)}) async-start(), calls=%async_computation.2 | async-start | bytes 2097152 | tf_op jit(solution)/shard_map/psum | solution.py:84
  162.1 40.1 %copy-start.1 = (f32[12,16,8,128]{3,2,1,0:T(8,128)}, f32[12,16,8,128]{3,2,1,0:T(8,128)S(1)}, u32[]{:S(2)}) copy-start(f32[12,16,8,128]{3,2,1,0:T(8,128)S(1)} %fusion.31) | copy-start | bytes 2359300
Sparse Core Ops, SparseCore 0:
  40.0 27.6 reduce-scatter.1
  71.2 78.2 all-reduce.4
where the time goes:
time: 209 us
  waiting for transfers between devices  118 us (56%)
  blocking collectives  46.3 us (22%)
  matrix products  15.1 us (7%)
  between operations  14.4 us (7%)
  starting transfers between devices  8.51 us (4%)
  local copies, waits for them, and re-layouts  5.35 us (3%)
    psum x1, waiting for transfers between devices, on_device(): core_block = lax.psum(core_block, 'gy')  77.8 us
    psum x1, blocking collectives, on_device(): miss, mass = lax.psum((miss_local, mass_local), ('gx', 'gy'))  38.9 us
    reduce_scatter x1, waiting for transfers between devices, on_device(): lax.psum_scatter(jnp.einsum('xa,xyk->ayk', columns, packed, precision=HIG...  27.8 us
    ppermute x2, waiting for transfers between devices, padded_2(): after = lax.ppermute(first, axis, down)  8.07 us
    all_gather x1, blocking collectives, on_device(): lax.all_gather(mixed_y, 'gx', axis=0, tiled=True)  7.32 us
    ppermute x2, starting transfers between devices, padded_2(): before = lax.ppermute(last, axis, up)  5.85 us
    dot_general x2, matrix products, reaction(): return jnp.einsum('vw,wxyz->vxyz', mixing, rate_terms, precision=HIGH)  4.55 us
  transfers between devices with their start and end apart: 6, of which 5 were waited for; matrix products, arithmetic and copies ran while one was open for 1% of the time, Pallas kernels for 0%

commit v1 on v0

--- a/solution.py
+++ b/solution.py
@@ -81,7 +81,11 @@
         tiled=True,
     )
     core_block = jnp.einsum("ayk,yb->abk", part_x, basis_y, precision=HIGH)
-    core_block = lax.psum(core_block, "gy")
+    core_block = core_block
+    for hop in (1, 2, 4):
+        core_block = core_block + lax.ppermute(
+            core_block, "gy", [(dev, dev ^ hop) for dev in range(8)]
+        )
     mixed_y = jnp.einsum("abk,yb->ayk", core_block, basis_y, precision=HIGH)
     columns = basis_x
     decoded = jnp.einsum(

time: 209 us -> 223 us (1.067)
  waiting for transfers between devices: 118 us -> 129 us
  starting transfers between devices: 8.51 us -> 14.1 us
  matrix products: 15.1 us -> 12.8 us
    ppermute x0 -> x3, waiting for transfers between devices: none -> 88.5 us  [on_device(): lax.ppermute(core_block, 'gy', [(dev, dev ^ hop) for dev in range(8)])]
    psum x1 -> x0, waiting for transfers between devices: 77.8 us -> none  [on_device(): core_block = lax.psum(core_block, 'gy')]
    ppermute x0 -> x3, starting transfers between devices: none -> 5.6 us  [on_device(): lax.ppermute(core_block, 'gy', [(dev, dev ^ hop) for dev in range(8)])]
  transfers between devices with their start and end apart: 6 -> 8, of which waited for: 5 -> 7; matrix products, arithmetic and copies ran while one was open for 1% -> 1% of each run, Pallas kernels for 0% -> 0%
where the time goes in v1:
time: 223 us
  waiting for transfers between devices  129 us (58%)
  blocking collectives  45.9 us (21%)
  between operations  14.4 us (6%)
  starting transfers between devices  14.1 us (6%)
  matrix products  12.8 us (6%)
  local copies, waits for them, and re-layouts  5.4 us (2%)
    ppermute x3, waiting for transfers between devices, on_device(): lax.ppermute(core_block, 'gy', [(dev, dev ^ hop) for dev in range(8)])  88.5 us
    psum x1, blocking collectives, on_device(): miss, mass = lax.psum((miss_local, mass_local), ('gx', 'gy'))  39.1 us
    reduce_scatter x1, waiting for transfers between devices, on_device(): lax.psum_scatter(jnp.einsum('xa,xyk->ayk', columns, packed, precision=HIG...  27.8 us
    ppermute x2, waiting for transfers between devices, padded_2(): after = lax.ppermute(first, axis, down)  8.07 us
    all_gather x1, blocking collectives, on_device(): lax.all_gather(mixed_y, 'gx', axis=0, tiled=True)  6.78 us
    ppermute x2, starting transfers between devices, padded_2(): before = lax.ppermute(last, axis, up)  5.85 us
    ppermute x3, starting transfers between devices, on_device(): lax.ppermute(core_block, 'gy', [(dev, dev ^ hop) for dev in range(8)])  5.6 us
    dot_general x2, matrix products, reaction(): return jnp.einsum('vw,wxyz->vxyz', mixing, rate_terms, precision=HIGH)  4.55 us
  transfers between devices with their start and end apart: 8, of which 7 were waited for; matrix products, arithmetic and copies ran while one was open for 1% of the time, Pallas kernels for 0%

profile of v1, /device:TPU:0, one launch (start us, length us, event | category | flops | bytes accessed | tf_op | source)
XLA Modules:
  0.0 223.1 jit_solution(2104366885545758304)
XLA Ops:
  7.2 1.0 fusion.61
  8.3 2.4 %collective-permute-start = (f32[12,2,8,128]{3,0,2,1:T(8,128)S(1)}, f32[12,2,8,128]{3,0,2,1:T(8,128)S(1)}, u32[]{:S(2)}, u32[]{:S(2)}) collective-permute-start(f32[12,2,8,128]{3,0,2,1:T(8,128)S(1)} %copy.53), channel_id=1, source_target_pairs={{0,8},{8,16},{16,24},{1,9},{9,17},{17,25},{2,10},{10,18},{18,26},{... | collective-permute-start | bytes 294920 | tf_op jit(solution)/shard_map/ppermute | solution.py:16
  10.8 1.3 collective-permute-start.1
  12.6 3.5 %collective-permute-done.1 = f32[12,2,8,128]{3,0,2,1:T(8,128)S(1)} collective-permute-done((f32[12,2,8,128]{3,0,2,1:T(8,128)S(1)}, f32[12,2,8,128]{3,0,2,1:T(8,128)S(1)}, u32[]{:S(2)}, u32[]{:S(2)}) %collective-permute-start.1) | collective-permute-done | bytes 98336 | tf_op jit(solution)/shard_map/ppermute | solution.py:17
  16.2 3.4 %collective-permute-start.2 = (f32[12,20,2,128]{3,0,2,1:T(8,128)S(1)}, f32[12,20,2,128]{3,0,2,1:T(8,128)S(1)}, u32[]{:S(2)}, u32[]{:S(2)}) collective-permute-start(f32[12,20,2,128]{3,0,2,1:T(8,128)S(1)} %get-tuple-element.13), channel_id=1, source_target_pairs={{0,1},{1,2},{2,3},{3,4},{4,5},{5,6},{6,7},{8,9},{9,10},{10,11},{11... | collective-permute-start | bytes 737288 | tf_op jit(solution)/shard_map/ppermute | solution.py:16
  19.6 1.3 collective-permute-start.3
  21.0 4.2 %collective-permute-done.2 = f32[12,20,2,128]{3,0,2,1:T(8,128)S(1)} collective-permute-done((f32[12,20,2,128]{3,0,2,1:T(8,128)S(1)}, f32[12,20,2,128]{3,0,2,1:T(8,128)S(1)}, u32[]{:S(2)}, u32[]{:S(2)}) %collective-permute-start.2) | collective-permute-done | bytes 245792 | tf_op jit(solution)/shard_map/ppermute | solution.py:16
  25.2 4.6 %collective-permute-done.3 = f32[12,20,2,128]{3,0,2,1:T(8,128)S(1)} collective-permute-done((f32[12,20,2,128]{3,0,2,1:T(8,128)S(1)}, f32[12,20,2,128]{3,0,2,1:T(8,128)S(1)}, u32[]{:S(2)}, u32[]{:S(2)}) %collective-permute-start.3) | collective-permute-done | bytes 245792 | tf_op jit(solution)/shard_map/ppermute | solution.py:17
  30.1 2.3 %fusion.8 = f32[12,18,10,128]{3,0,2,1:T(8,128)S(1)} fusion(f32[12,20,12,128]{3,0,2,1:T(8,128)S(1)} %pad_maximum_fusion, f32[12,20,8,128]{3,0,2,1:T(8,128)S(1)} %constant_dynamic-update-slice_fusion, f32[12,20,2,128]{3,0,2,1:T(8,128)S(1)} %collective-permute-done.2, f32[12,20,2,128]{3,0,2,1:T(8,128)S(1)} %collective-permute-done.3, ...), kind=kOutput, calls=%fused_computation.14 | convolution fusion | flops 44236800 | bytes 11096576 | tf_op jit(solution)/shard_map/vw,wxyz->vxyz/dot_general | solution.py:38
  32.6 2.2 fusion.23
  34.8 1.0 fusion.47
  35.8 0.7 fusion.55
  36.5 0.5 copy.24
  37.1 1.7 fusion.36
  38.7 1.1 copy.55
  39.9 27.8 %reduce-scatter.2.cloned.1.call-done = f32[16,8,192]{2,1,0:T(8,128)} async-done(((f32[64,8,192]{2,1,0:T(8,128)}), f32[16,8,192]{2,1,0:T(8,128)}) %reduce-scatter.2.cloned.1.call-update) | async-done | bytes 98320 | tf_op jit(solution)/shard_map/reduce_scatter | solution.py:77
  67.7 1.9 convolution_bitcast_fusion
  69.6 1.6 collective-permute-start.4
  71.2 23.2 %collective-permute-done.4 = f32[16,64,192]{2,1,0:T(8,128)S(1)} collective-permute-done((f32[16,64,192]{2,1,0:T(8,128)S(1)}, f32[16,64,192]{2,1,0:T(8,128)S(1)}, u32[]{:S(2)}, u32[]{:S(2)}) %collective-permute-start.4) | collective-permute-done | bytes 786464 | tf_op jit(solution)/shard_map/ppermute | solution.py:86
  94.6 1.6 collective-permute-start.5
  96.1 22.4 %collective-permute-done.5 = f32[16,64,192]{2,1,0:T(8,128)S(1)} collective-permute-done((f32[16,64,192]{2,1,0:T(8,128)S(1)}, f32[16,64,192]{2,1,0:T(8,128)S(1)}, u32[]{:S(2)}, u32[]{:S(2)}) %collective-permute-start.5) | collective-permute-done | bytes 786464 | tf_op jit(solution)/shard_map/ppermute | solution.py:86
  118.7 2.5 %collective-permute-start.6 = (f32[16,64,192]{2,1,0:T(8,128)S(1)}, f32[16,64,192]{2,1,0:T(8,128)S(1)}, u32[]{:S(2)}, u32[]{:S(2)}) collective-permute-start(f32[16,64,192]{2,1,0:T(8,128)S(1)} %add.135), channel_id=1, source_target_pairs={{0,4},{1,5},{2,6},{3,7},{4,0},{5,1},{6,2},{7,3},{8,12},{9,13},{10,... | collective-permute-start | bytes 2359304 | tf_op jit(solution)/shard_map/ppermute | solution.py:86
  121.2 1.1 copy.27
  122.3 42.9 %collective-permute-done.6 = f32[16,64,192]{2,1,0:T(8,128)S(1)} collective-permute-done((f32[16,64,192]{2,1,0:T(8,128)S(1)}, f32[16,64,192]{2,1,0:T(8,128)S(1)}, u32[]{:S(2)}, u32[]{:S(2)}) %collective-permute-start.6) | collective-permute-done | bytes 786464 | tf_op jit(solution)/shard_map/ppermute | solution.py:86
  165.1 0.7 fusion.26
  165.9 6.8 %all_gather.3 = f32[64,8,192]{2,0,1:T(8,128)S(1)} all-gather(f32[16,8,192]{2,0,1:T(8,128)S(1)} %bitcast.65), channel_id=1, replica_groups=mesh['gx'=4,'gy'=8] {'gx'}, dimensions={0}, use_global_device_ids=true | all-gather | bytes 491520 | tf_op jit(solution)/shard_map/all_gather | solution.py:92
  173.4 0.6 copy.34
  174.0 1.0 fusion.53
  175.0 0.9 fusion.33
  176.0 0.7 multiply_reduce_fusion
  176.6 39.1 %all-reduce.2 = (f32[12]{0:T(128)S(1)}, f32[12]{0:T(128)S(1)}) all-reduce(f32[12]{0:T(128)S(1)} %get-tuple-element.10, f32[12]{0:T(128)S(1)} %get-tuple-element.9), channel_id=1, replica_groups=mesh['gx'=4,'gy'=8] {'gx','gy'}, use_global_device_ids=true, to_apply=%region_2.3 | all-reduce | flops 24 | bytes 192 | tf_op jit(solution)/shard_map/psum | solution.py:100
  215.8 0.5 fusion.59
  (42 shorter events, 2.3 us)
Async XLA Ops:
  7.2 27.6 %copy-start = (f32[128,32]{0,1:T(8,128)S(1)}, f32[128,32]{0,1:T(8,128)}, u32[]{:S(2)}) copy-start(f32[128,32]{0,1:T(8,128)} %param.16) | copy-start | bytes 49156
  7.2 4.9 %copy-start.2 = (f32[12,16,8,128]{3,2,1,0:T(8,128)S(1)}, f32[12,16,8,128]{3,2,1,0:T(8,128)}, u32[]{:S(2)}) copy-start(f32[12,16,8,128]{3,2,1,0:T(8,128)} %param.9) | copy-start | bytes 2359300
  7.2 60.5 %reduce-scatter.2.cloned.1.call-start = ((), (), s32[]{:S(2)}) async-start(), calls=%async_computation.1 | async-start | bytes 655360 | tf_op jit(solution)/shard_map/reduce_scatter | solution.py:77
  8.3 3.8 %collective-permute-start = (f32[12,2,8,128]{3,0,2,1:T(8,128)S(1)}, f32[12,2,8,128]{3,0,2,1:T(8,128)S(1)}, u32[]{:S(2)}, u32[]{:S(2)}) collective-permute-start(f32[12,2,8,128]{3,0,2,1:T(8,128)S(1)} %copy.53), channel_id=1, source_target_pairs={{0,8},{8,16},{16,24},{1,9},{9,17},{17,25},{2,10},{10,18},{18,26},{... | collective-permute-start | bytes 294920 | tf_op jit(solution)/shard_map/ppermute | solution.py:16
  10.8 5.3 %collective-permute-start.1 = (f32[12,2,8,128]{3,0,2,1:T(8,128)S(1)}, f32[12,2,8,128]{3,0,2,1:T(8,128)S(1)}, u32[]{:S(2)}, u32[]{:S(2)}) collective-permute-start(f32[12,2,8,128]{3,0,2,1:T(8,128)S(1)} %copy.54), channel_id=1, source_target_pairs={{8,0},{16,8},{24,16},{9,1},{17,9},{25,17},{10,2},{18,10},{26,18},{... | collective-permute-start | bytes 294920 | tf_op jit(solution)/shard_map/ppermute | solution.py:17
  12.1 8.8 %copy-start.7 = (f32[12]{0:T(128)S(1)}, f32[12]{0:T(128)}, u32[]{:S(2)}) copy-start(f32[12]{0:T(128)} %param.12) | copy-start | bytes 148
  16.2 9.0 %collective-permute-start.2 = (f32[12,20,2,128]{3,0,2,1:T(8,128)S(1)}, f32[12,20,2,128]{3,0,2,1:T(8,128)S(1)}, u32[]{:S(2)}, u32[]{:S(2)}) collective-permute-start(f32[12,20,2,128]{3,0,2,1:T(8,128)S(1)} %get-tuple-element.13), channel_id=1, source_target_pairs={{0,1},{1,2},{2,3},{3,4},{4,5},{5,6},{6,7},{8,9},{9,10},{10,11},{11... | collective-permute-start | bytes 737288 | tf_op jit(solution)/shard_map/ppermute | solution.py:16
  19.6 10.2 %collective-permute-start.3 = (f32[12,20,2,128]{3,0,2,1:T(8,128)S(1)}, f32[12,20,2,128]{3,0,2,1:T(8,128)S(1)}, u32[]{:S(2)}, u32[]{:S(2)}) collective-permute-start(f32[12,20,2,128]{3,0,2,1:T(8,128)S(1)} %get-tuple-element.14), channel_id=1, source_target_pairs={{1,0},{2,1},{3,2},{4,3},{5,4},{6,5},{7,6},{9,8},{10,9},{11,10},{12... | collective-permute-start | bytes 737288 | tf_op jit(solution)/shard_map/ppermute | solution.py:17
  21.0 9.1 %copy-start.6 = (f32[12,12]{1,0:T(8,128)S(1)}, f32[12,12]{1,0:T(8,128)}, u32[]{:S(2)}) copy-start(f32[12,12]{1,0:T(8,128)} %param.13) | copy-start | bytes 1732
  21.0 9.1 %copy-start.8 = (f32[12]{0:T(128)S(1)}, f32[12]{0:T(128)}, u32[]{:S(2)}) copy-start(f32[12]{0:T(128)} %param.11) | copy-start | bytes 148
  21.0 9.1 %copy-start.9 = (f32[12]{0:T(128)S(1)}, f32[12]{0:T(128)}, u32[]{:S(2)}) copy-start(f32[12]{0:T(128)} %param.10) | copy-start | bytes 148
  34.8 1.0 copy-start.5
  35.8 1.3 copy-start.3
  37.1 30.6 %copy-start.4 = (f32[8,64]{1,0:T(8,128)S(1)}, f32[8,64]{1,0:T(8,128)}, u32[]{:S(2)}) copy-start(f32[8,64]{1,0:T(8,128)} %param.15) | copy-start | bytes 6148
  69.6 24.8 %collective-permute-start.4 = (f32[16,64,192]{2,1,0:T(8,128)S(1)}, f32[16,64,192]{2,1,0:T(8,128)S(1)}, u32[]{:S(2)}, u32[]{:S(2)}) collective-permute-start(f32[16,64,192]{2,1,0:T(8,128)S(1)} %convolution_bitcast_fusion), channel_id=1, source_target_pairs={{0,1},{1,0},{2,3},{3,2},{4,5},{5,4},{6,7},{7,6},{8,9},{9,8},{10,11... | collective-permute-start | bytes 2359304 | tf_op jit(solution)/shard_map/ppermute | solution.py:86
  94.6 23.9 %collective-permute-start.5 = (f32[16,64,192]{2,1,0:T(8,128)S(1)}, f32[16,64,192]{2,1,0:T(8,128)S(1)}, u32[]{:S(2)}, u32[]{:S(2)}) collective-permute-start(f32[16,64,192]{2,1,0:T(8,128)S(1)} %add.134), channel_id=1, source_target_pairs={{0,2},{1,3},{2,0},{3,1},{4,6},{5,7},{6,4},{7,5},{8,10},{9,11},{10,... | collective-permute-start | bytes 2359304 | tf_op jit(solution)/shard_map/ppermute | solution.py:86
  118.7 46.5 %collective-permute-start.6 = (f32[16,64,192]{2,1,0:T(8,128)S(1)}, f32[16,64,192]{2,1,0:T(8,128)S(1)}, u32[]{:S(2)}, u32[]{:S(2)}) collective-permute-start(f32[16,64,192]{2,1,0:T(8,128)S(1)} %add.135), channel_id=1, source_target_pairs={{0,4},{1,5},{2,6},{3,7},{4,0},{5,1},{6,2},{7,3},{8,12},{9,13},{10,... | collective-permute-start | bytes 2359304 | tf_op jit(solution)/shard_map/ppermute | solution.py:86
  176.0 40.3 %copy-start.1 = (f32[12,16,8,128]{3,2,1,0:T(8,128)}, f32[12,16,8,128]{3,2,1,0:T(8,128)S(1)}, u32[]{:S(2)}) copy-start(f32[12,16,8,128]{3,2,1,0:T(8,128)S(1)} %fusion.33) | copy-start | bytes 2359300
Sparse Core Ops, SparseCore 0:
  40.0 27.6 reduce-scatter.1
